TPU v7x, 256 devices: a whole 4x4x8 slice. The times are simulated.
256 devices in a mesh: row: 64 (over z, x, core), col: 4 (over y).
Axes of the slice: x: 4, y: 4, z: 8, core: 2. Of those that a mesh axis runs over, the one named last changes fastest.
Arguments:
- right_sides: float32 [4, 256, 128, 128], P(None, 'row'), may hold values from -6 to 6
- inverse_diag: float32 [4, 256, 128, 128], P(None, 'row', 'col'), may hold values from -1 to 2
- lower_blocks: float32 [3, 256, 16, 128, 128], P(None, 'row', None, 'col'), may hold values from -0.09375 to 0.09375
- depends_on: int32 [3, 256, 16], replicated, may hold values from 0 to 255, as said below
Outputs:
- solution: float32 [4, 256, 128, 128], P(None, 'row', 'col')
Inputs may be any that keep to these rules, and one draw needn't show every extreme that they name: `depends_on`: in each level, the supernodes of one device along row name the supernodes of any one device along row at most 2 times in all, and some pair of devices reaches 2 in every level.
All inputs are finite; a program needn't handle non-finite values.
Results may differ from a plain program's by a relative error of at most 0.0001.
Values sent between devices are 32-bit elements; how exact they have to be, the bound alone decides.
A program may use at most 64 MiB of HBM per device.

v0:
```python
import jax
import jax.numpy as jnp
from jax import lax
from jax.sharding import PartitionSpec as P

exact_mode = lax.Precision.HIGHEST


def fetch_blocks(previous, wanted):
    shard_rows = lax.all_gather(previous, "row", axis=0, tiled=True)
    chooser = (wanted[:, None] == jnp.arange(shard_rows.shape[0], dtype=jnp.int32)[None, :]).astype(
        jnp.float32
    )
    return jnp.einsum("en,nrk->erk", chooser, shard_rows, precision=exact_mode)


def return_terms(terms, wanted, local_count):
    owners = (
        jnp.arange(local_count * lax.axis_size("row"), dtype=jnp.int32)[:, None] == wanted[None, :]
    ).astype(jnp.float32)
    return lax.psum_scatter(
        jnp.einsum("me,erk->mrk", owners, terms, precision=exact_mode),
        "row",
        scatter_dimension=0,
        tiled=True,
    )


def forward_update(partial_value):
    return lax.psum(partial_value, "col")


def backward_solve(inverse_level, rest):
    partial_value = jnp.einsum("jab,jak->jbk", inverse_level, rest, precision=exact_mode)
    return lax.psum(partial_value, "col")


def on_device(right_sides, inverse_diag, lower_blocks, depends_on):
    levels, local_count, width, columns = right_sides.shape
    share = inverse_diag.shape[2]
    fan_in = lower_blocks.shape[2]
    my_row = lax.axis_index("row")
    my_col = lax.axis_index("col")
    entries = local_count * fan_in
    wanted_all = [
        lax.dynamic_slice_in_dim(
            depends_on[level_no], my_row * local_count, local_count, 0
        ).reshape(entries)
        for level_no in range(levels - 1)
    ]
    solved_here = [
        jnp.einsum("jab,jbk->jak", inverse_diag[0], right_sides[0], precision=exact_mode)
    ]
    for level_no in range(1, levels):
        picked = fetch_blocks(solved_here[-1], wanted_all[level_no - 1])
        partial_value = jnp.einsum(
            "jdba,jdbk->jak",
            lower_blocks[level_no - 1],
            picked.reshape(local_count, fan_in, share, columns),
            precision=exact_mode,
        )
        update = forward_update(partial_value)
        residual = right_sides[level_no] - update
        solved_here.append(
            jnp.einsum("jab,jbk->jak", inverse_diag[level_no], residual, precision=exact_mode)
        )
    full_sol = backward_solve(inverse_diag[levels - 1], solved_here[levels - 1])
    pieces = [lax.dynamic_slice_in_dim(full_sol, my_col * share, share, 1)]
    for level_no in range(levels - 2, -1, -1):
        terms = jnp.einsum(
            "jdba,jak->jdbk", lower_blocks[level_no], full_sol, precision=exact_mode
        ).reshape(entries, share, columns)
        returned = return_terms(terms, wanted_all[level_no], local_count)
        rest = solved_here[level_no] - returned
        full_sol = backward_solve(inverse_diag[level_no], rest)
        pieces.insert(0, lax.dynamic_slice_in_dim(full_sol, my_col * share, share, 1))
    return jnp.stack(pieces)


def solution(mesh):
    return jax.shard_map(
        on_device,
        mesh=mesh,
        in_specs=(
            P(None, "row", None, None),
            P(None, "row", "col", None),
            P(None, "row", None, "col", None),
            P(),
        ),
        out_specs=P(None, "row", "col", None),
        check_vma=False,
    )
```

profile of v0, /device:TPU:2, one launch (start us, length us, event | category | flops | bytes accessed | tf_op | source)
XLA Modules:
  0.0 1079.7 jit_solution(4726448590712107465)
XLA Ops:
  9.6 3.6 fusion.65
  13.2 77.8 %all-gather.4.cloned.1.call-done = f32[256,32,128]{2,1,0:T(8,128)} async-done(((f32[4,32,128]{2,1,0:T(8,128)}), f32[256,32,128]{2,1,0:T(8,128)}) %all-gather.4.cloned.1.call-update) | async-done | bytes 4194320 | tf_op jit(solution)/shard_map/all_gather | solution.py:10
  91.0 6.2 fusion.4
  97.2 3.0 convolution_bitcast_fusion.6
  101.2 44.4 %all-reduce.8.cloned.1.call-done = f32[4,128,128]{1,2,0:T(8,128)} async-done(((f32[4,128,128]{1,2,0:T(8,128)}), f32[4,128,128]{1,2,0:T(8,128)}) %all-reduce.8.cloned.1.call-update) | async-done | bytes 262160 | tf_op jit(solution)/shard_map/psum | solution.py:30
  145.6 2.1 convolution_bitcast_fusion.8
  148.3 78.8 %all-gather.6.cloned.1.call-done = f32[256,32,128]{2,1,0:T(8,128)} async-done(((f32[4,32,128]{2,1,0:T(8,128)}), f32[256,32,128]{2,1,0:T(8,128)}) %all-gather.6.cloned.1.call-update) | async-done | bytes 4194320 | tf_op jit(solution)/shard_map/all_gather | solution.py:10
  227.1 6.1 fusion.2
  233.2 3.0 convolution_bitcast_fusion.5
  236.4 45.2 %all-reduce.10.cloned.1.call-done = f32[4,128,128]{1,2,0:T(8,128)} async-done(((f32[4,128,128]{1,2,0:T(8,128)}), f32[4,128,128]{1,2,0:T(8,128)}) %all-reduce.10.cloned.1.call-update) | async-done | bytes 262160 | tf_op jit(solution)/shard_map/psum | solution.py:30
  281.6 2.1 convolution_bitcast_fusion.7
  284.3 78.3 %all-gather.8.cloned.1.call-done = f32[256,32,128]{2,1,0:T(8,128)} async-done(((f32[4,32,128]{2,1,0:T(8,128)}), f32[256,32,128]{2,1,0:T(8,128)}) %all-gather.8.cloned.1.call-update) | async-done | bytes 4194320 | tf_op jit(solution)/shard_map/all_gather | solution.py:10
  362.6 6.1 fusion
  368.7 4.4 convolution_bitcast_fusion.4
  375.0 43.5 %all-reduce.12.cloned.1.call-done = f32[4,128,128]{1,2,0:T(8,128)} async-done(((f32[4,128,128]{1,2,0:T(8,128)}), f32[4,128,128]{1,2,0:T(8,128)}) %all-reduce.12.cloned.1.call-update) | async-done | bytes 262160 | tf_op jit(solution)/shard_map/psum | solution.py:30
  422.0 46.8 %all-reduce.14.cloned.1.call-done = f32[4,128,128]{1,2,0:T(8,128)} async-done(((f32[4,128,128]{1,2,0:T(8,128)}), f32[4,128,128]{1,2,0:T(8,128)}) %all-reduce.14.cloned.1.call-update) | async-done | bytes 262160 | tf_op jit(solution)/shard_map/psum | solution.py:35
  470.8 2.3 fusion.16
  473.1 4.4 copy.45
  477.6 143.6 %reduce-scatter.4.cloned.1.call-done = f32[4,32,128]{2,1,0:T(8,128)} async-done(((f32[256,32,128]{2,1,0:T(8,128)}), f32[4,32,128]{2,1,0:T(8,128)}) %reduce-scatter.4.cloned.1.call-update) | async-done | bytes 65552 | tf_op jit(solution)/shard_map/reduce_scatter | solution.py:21
  621.1 2.1 convolution_bitcast_fusion.2
  623.5 46.0 %all-reduce.16.cloned.1.call-done = f32[4,128,128]{1,2,0:T(8,128)} async-done(((f32[4,128,128]{1,2,0:T(8,128)}), f32[4,128,128]{1,2,0:T(8,128)}) %all-reduce.16.cloned.1.call-update) | async-done | bytes 262160 | tf_op jit(solution)/shard_map/psum | solution.py:35
  669.6 1.9 fusion.8
  671.5 2.3 fusion.14
  673.9 4.4 copy.49
  678.3 143.5 %reduce-scatter.6.cloned.1.call-done = f32[4,32,128]{2,1,0:T(8,128)} async-done(((f32[256,32,128]{2,1,0:T(8,128)}), f32[4,32,128]{2,1,0:T(8,128)}) %reduce-scatter.6.cloned.1.call-update) | async-done | bytes 65552 | tf_op jit(solution)/shard_map/reduce_scatter | solution.py:21
  821.8 2.1 convolution_bitcast_fusion.1
  824.3 46.0 %all-reduce.18.cloned.1.call-done = f32[4,128,128]{1,2,0:T(8,128)} async-done(((f32[4,128,128]{1,2,0:T(8,128)}), f32[4,128,128]{1,2,0:T(8,128)}) %all-reduce.18.cloned.1.call-update) | async-done | bytes 262160 | tf_op jit(solution)/shard_map/psum | solution.py:35
  872.3 2.3 fusion.12
  874.6 4.4 copy.53
  879.1 143.5 %reduce-scatter.8.cloned.1.call-done = f32[4,32,128]{2,1,0:T(8,128)} async-done(((f32[256,32,128]{2,1,0:T(8,128)}), f32[4,32,128]{2,1,0:T(8,128)}) %reduce-scatter.8.cloned.1.call-update) | async-done | bytes 65552 | tf_op jit(solution)/shard_map/reduce_scatter | solution.py:21
  1022.6 2.1 convolution_bitcast_fusion
  1025.5 45.5 %all-reduce.20.cloned.1.call-done = f32[4,128,128]{1,2,0:T(8,128)} async-done(((f32[4,128,128]{1,2,0:T(8,128)}), f32[4,128,128]{1,2,0:T(8,128)}) %all-reduce.20.cloned.1.call-update) | async-done | bytes 262160 | tf_op jit(solution)/shard_map/psum | solution.py:35
  (73 shorter events, 17.9 us)
Async XLA Ops:
  6.5 84.4 %all-gather.4.cloned.1.call-start = ((), (), s32[]{:S(2)}) async-start(), calls=%async_computation.3 | async-start | bytes 4259840 | tf_op jit(solution)/shard_map/all_gather | solution.py:10
  8.5 137.1 %all-reduce.8.cloned.1.call-start = ((), (), s32[]{:S(2)}) async-start(), calls=%async_computation.4 | async-start | bytes 524288 | tf_op jit(solution)/shard_map/psum | solution.py:30
  13.2 87.1 %copy-start.5 = (f32[4,4,128,128]{3,2,1,0:T(8,128)S(1)}, f32[4,4,128,128]{3,2,1,0:T(8,128)}, u32[]{:S(2)}) copy-start(f32[4,4,128,128]{3,2,1,0:T(8,128)} %param.4) | copy-start | bytes 3145732
  91.0 6.2 copy-start.6
  97.2 48.4 %copy-start.4 = (f32[4,4,32,128]{3,2,1,0:T(8,128)S(1)}, f32[4,4,32,128]{3,2,1,0:T(8,128)}, u32[]{:S(2)}) copy-start(f32[4,4,32,128]{3,2,1,0:T(8,128)} %param.5) | copy-start | bytes 786436
  100.2 126.9 %all-gather.6.cloned.1.call-start = ((), (), s32[]{:S(2)}) async-start(), calls=%async_computation.5 | async-start | bytes 4259840 | tf_op jit(solution)/shard_map/all_gather | solution.py:10
  147.7 133.9 %all-reduce.10.cloned.1.call-start = ((), (), s32[]{:S(2)}) async-start(), calls=%async_computation.6 | async-start | bytes 524288 | tf_op jit(solution)/shard_map/psum | solution.py:30
  236.3 126.3 %all-gather.8.cloned.1.call-start = ((), (), s32[]{:S(2)}) async-start(), calls=%async_computation.7 | async-start | bytes 4259840 | tf_op jit(solution)/shard_map/all_gather | solution.py:10
  283.7 134.8 %all-reduce.12.cloned.1.call-start = ((), (), s32[]{:S(2)}) async-start(), calls=%async_computation.8 | async-start | bytes 524288 | tf_op jit(solution)/shard_map/psum | solution.py:30
  368.7 100.1 %copy-start = (f32[3,4,16,32,128]{4,3,2,1,0:T(8,128)S(1)}, f32[3,4,16,32,128]{4,3,2,1,0:T(8,128)}, u32[]{:S(2)}) copy-start(f32[3,4,16,32,128]{4,3,2,1,0:T(8,128)} %param.6) | copy-start | bytes 9437188
  373.1 95.7 %all-reduce.14.cloned.1.call-start = ((), (), s32[]{:S(2)}) async-start(), calls=%async_computation.9 | async-start | bytes 524288 | tf_op jit(solution)/shard_map/psum | solution.py:35
  421.4 199.7 %reduce-scatter.4.cloned.1.call-start = ((), (), s32[]{:S(2)}) async-start(), calls=%async_computation.10 | async-start | bytes 4259840 | tf_op jit(solution)/shard_map/reduce_scatter | solution.py:21
  477.5 143.6 %copy-start.8 = (f32[4,32,128]{2,1,0:T(8,128)S(1)}, f32[4,32,128]{2,1,0:T(8,128)}, u32[]{:S(2)}) copy-start(f32[4,32,128]{2,1,0:T(8,128)} %convolution_bitcast_fusion.7) | copy-start | bytes 196612
  477.5 192.0 %all-reduce.16.cloned.1.call-start = ((), (), s32[]{:S(2)}) async-start(), calls=%async_computation.11 | async-start | bytes 524288 | tf_op jit(solution)/shard_map/psum | solution.py:35
  623.3 198.6 %reduce-scatter.6.cloned.1.call-start = ((), (), s32[]{:S(2)}) async-start(), calls=%async_computation.12 | async-start | bytes 4259840 | tf_op jit(solution)/shard_map/reduce_scatter | solution.py:21
  678.2 143.6 %copy-start.7 = (f32[4,32,128]{2,1,0:T(8,128)S(1)}, f32[4,32,128]{2,1,0:T(8,128)}, u32[]{:S(2)}) copy-start(f32[4,32,128]{2,1,0:T(8,128)} %convolution_bitcast_fusion.8) | copy-start | bytes 196612
  678.3 192.0 %all-reduce.18.cloned.1.call-start = ((), (), s32[]{:S(2)}) async-start(), calls=%async_computation.13 | async-start | bytes 524288 | tf_op jit(solution)/shard_map/psum | solution.py:35
  824.0 198.6 %reduce-scatter.8.cloned.1.call-start = ((), (), s32[]{:S(2)}) async-start(), calls=%async_computation.14 | async-start | bytes 4259840 | tf_op jit(solution)/shard_map/reduce_scatter | solution.py:21
  879.0 143.6 %copy-start.9 = (f32[4,32,128]{2,1,0:T(8,128)S(1)}, f32[4,32,128]{2,1,0:T(8,128)}, u32[]{:S(2)}) copy-start(f32[4,32,128]{2,1,0:T(8,128)} %fusion.22) | copy-start | bytes 196612
  879.0 145.8 %copy-start.1 = (f32[4,128,128]{1,2,0:T(8,128)S(1)}, f32[4,128,128]{1,2,0:T(8,128)}, u32[]{:S(2)}) copy-start(f32[4,128,128]{1,2,0:T(8,128)} %all-reduce.14.cloned.1.call-done) | copy-start | bytes 786436
  879.0 146.0 %copy-start.2 = (f32[4,128,128]{1,2,0:T(8,128)S(1)}, f32[4,128,128]{1,2,0:T(8,128)}, u32[]{:S(2)}) copy-start(f32[4,128,128]{1,2,0:T(8,128)} %all-reduce.16.cloned.1.call-done) | copy-start | bytes 786436
  879.0 146.3 %copy-start.3 = (f32[4,128,128]{1,2,0:T(8,128)S(1)}, f32[4,128,128]{1,2,0:T(8,128)}, u32[]{:S(2)}) copy-start(f32[4,128,128]{1,2,0:T(8,128)} %all-reduce.18.cloned.1.call-done) | copy-start | bytes 786436
  879.0 192.0 %all-reduce.20.cloned.1.call-start = ((), (), s32[]{:S(2)}) async-start(), calls=%async_computation.15 | async-start | bytes 524288 | tf_op jit(solution)/shard_map/psum | solution.py:35
Sparse Core Ops, SparseCore 0:
  10.1 80.7 all-gather.3
  100.3 45.2 all-reduce.7
  148.7 78.3 all-gather.5
  236.4 45.1 all-reduce.9
  284.2 78.3 all-gather.7
  373.2 45.2 all-reduce.11
  421.5 47.2 all-reduce.13
  477.6 143.4 reduce-scatter.3
  623.6 45.9 all-reduce.15
  678.4 143.4 reduce-scatter.5
  824.3 45.9 all-reduce.17
  879.1 143.4 reduce-scatter.7
  1025.0 45.9 all-reduce.19
where the time goes:
time: 1090 us; the launch traced here: 1080 us
  waiting for transfers between devices  983 us (90%)
  matrix products  57.1 us (5%)
  local copies, waits for them, and re-layouts  22.8 us (2%)
  between operations  13.7 us (1%)
    reduce_scatter x3, waiting for transfers between devices, return_terms(): lax.psum_scatter(jnp.einsum('me,erk->mrk', owners, terms, precision=exact...  431 us
    all_gather x3, waiting for transfers between devices, fetch_blocks(): shard_rows = lax.all_gather(previous, 'row', axis=0, tiled=True)  235 us
    psum x4, waiting for transfers between devices, backward_solve(): return lax.psum(partial_value, 'col')  184 us
    psum x3, waiting for transfers between devices, forward_update(): return lax.psum(partial_value, 'col')  133 us
  transfers between devices with their start and end apart: 13, of which 13 were waited for; matrix products, arithmetic and copies ran while one was open for 1% of the time, Pallas kernels for 0%

commit v1 on v0

--- a/solution.py
+++ b/solution.py
@@ -27,7 +27,7 @@
 
 
 def forward_update(partial_value):
-    return lax.psum(partial_value, "col")
+    return jnp.sum(lax.all_gather(partial_value, "col"), axis=0)
 
 
 def backward_solve(inverse_level, rest):

time: 1090 us -> 1030 us (0.945)
  waiting for transfers between devices: 983 us -> 921 us
    psum x3 -> x0, waiting for transfers between devices: 133 us -> none  [forward_update(): return lax.psum(partial_value, 'col')]
    all_gather x0 -> x3, waiting for transfers between devices: none -> 72.4 us  [forward_update(): return jnp.sum(lax.all_gather(partial_value, 'col'), axis=0)]
where the time goes in v1:
time: 1030 us; the launch traced here: 1020 us
  waiting for transfers between devices  921 us (89%)
  matrix products  53.8 us (5%)
  local copies, waits for them, and re-layouts  28.3 us (3%)
  between operations  13.7 us (1%)
    reduce_scatter x3, waiting for transfers between devices, return_terms(): lax.psum_scatter(jnp.einsum('me,erk->mrk', owners, terms, precision=exact...  431 us
    all_gather x3, waiting for transfers between devices, fetch_blocks(): shard_rows = lax.all_gather(previous, 'row', axis=0, tiled=True)  233 us
    psum x4, waiting for transfers between devices, backward_solve(): return lax.psum(partial_value, 'col')  184 us
    all_gather x3, waiting for transfers between devices, forward_update(): return jnp.sum(lax.all_gather(partial_value, 'col'), axis=0)  72.4 us
  transfers between devices with their start and end apart: 13, of which 13 were waited for; matrix products, arithmetic and copies ran while one was open for 1% of the time, Pallas kernels for 0%

profile of v1, /device:TPU:2, one launch (start us, length us, event | category | flops | bytes accessed | tf_op | source)
XLA Modules:
  0.0 1024.0 jit_solution(3448343678098977015)
XLA Ops:
  9.6 3.6 fusion.65
  13.2 77.8 %all-gather.10.cloned.1.call-done = f32[256,32,128]{2,1,0:T(8,128)} async-done(((f32[4,32,128]{2,1,0:T(8,128)}), f32[256,32,128]{2,1,0:T(8,128)}) %all-gather.10.cloned.1.call-update) | async-done | bytes 4194320 | tf_op jit(solution)/shard_map/all_gather | solution.py:10
  91.0 6.2 fusion.4
  97.2 2.3 convolution_bitcast_fusion.6
  101.3 24.2 %all-gather.16.cloned.1.call-done = f32[16,128,128]{2,1,0:T(8,128)} async-done(((f32[4,128,128]{2,1,0:T(8,128)}), f32[16,128,128]{2,1,0:T(8,128)}) %all-gather.16.cloned.1.call-update) | async-done | bytes 1048592 | tf_op jit(solution)/shard_map/all_gather | solution.py:30
  128.7 77.8 %all-gather.12.cloned.1.call-done = f32[256,32,128]{2,1,0:T(8,128)} async-done(((f32[4,32,128]{2,1,0:T(8,128)}), f32[256,32,128]{2,1,0:T(8,128)}) %all-gather.12.cloned.1.call-update) | async-done | bytes 4194320 | tf_op jit(solution)/shard_map/all_gather | solution.py:10
  206.4 6.1 fusion.2
  212.6 2.3 convolution_bitcast_fusion.5
  215.9 24.9 %all-gather.18.cloned.1.call-done = f32[16,128,128]{2,1,0:T(8,128)} async-done(((f32[4,128,128]{2,1,0:T(8,128)}), f32[16,128,128]{2,1,0:T(8,128)}) %all-gather.18.cloned.1.call-update) | async-done | bytes 1048592 | tf_op jit(solution)/shard_map/all_gather | solution.py:30
  244.0 77.8 %all-gather.14.cloned.1.call-done = f32[256,32,128]{2,1,0:T(8,128)} async-done(((f32[4,32,128]{2,1,0:T(8,128)}), f32[256,32,128]{2,1,0:T(8,128)}) %all-gather.14.cloned.1.call-update) | async-done | bytes 4194320 | tf_op jit(solution)/shard_map/all_gather | solution.py:10
  321.8 6.1 fusion
  327.9 4.4 convolution_bitcast_fusion.4
  335.9 23.3 %all-gather.20.cloned.1.call-done = f32[16,128,128]{2,1,0:T(8,128)} async-done(((f32[4,128,128]{2,1,0:T(8,128)}), f32[16,128,128]{2,1,0:T(8,128)}) %all-gather.20.cloned.1.call-update) | async-done | bytes 1048592 | tf_op jit(solution)/shard_map/all_gather | solution.py:30
  359.2 2.0 reduce_sum.29
  366.5 46.7 %all-reduce.5.cloned.1.call-done = f32[4,128,128]{1,2,0:T(8,128)} async-done(((f32[4,128,128]{1,2,0:T(8,128)}), f32[4,128,128]{1,2,0:T(8,128)}) %all-reduce.5.cloned.1.call-update) | async-done | bytes 262160 | tf_op jit(solution)/shard_map/psum | solution.py:35
  413.2 1.9 fusion.10
  415.1 2.3 fusion.16
  417.5 4.4 copy.57
  421.9 143.7 %reduce-scatter.4.cloned.1.call-done = f32[4,32,128]{2,1,0:T(8,128)} async-done(((f32[256,32,128]{2,1,0:T(8,128)}), f32[4,32,128]{2,1,0:T(8,128)}) %reduce-scatter.4.cloned.1.call-update) | async-done | bytes 65552 | tf_op jit(solution)/shard_map/reduce_scatter | solution.py:21
  565.6 2.1 convolution_bitcast_fusion.2
  568.0 45.9 %all-reduce.7.cloned.1.call-done = f32[4,128,128]{1,2,0:T(8,128)} async-done(((f32[4,128,128]{1,2,0:T(8,128)}), f32[4,128,128]{1,2,0:T(8,128)}) %all-reduce.7.cloned.1.call-update) | async-done | bytes 262160 | tf_op jit(solution)/shard_map/psum | solution.py:35
  615.8 2.3 fusion.14
  618.2 4.4 copy.61
  622.6 143.6 %reduce-scatter.6.cloned.1.call-done = f32[4,32,128]{2,1,0:T(8,128)} async-done(((f32[256,32,128]{2,1,0:T(8,128)}), f32[4,32,128]{2,1,0:T(8,128)}) %reduce-scatter.6.cloned.1.call-update) | async-done | bytes 65552 | tf_op jit(solution)/shard_map/reduce_scatter | solution.py:21
  766.3 2.1 convolution_bitcast_fusion.1
  768.7 45.9 %all-reduce.9.cloned.1.call-done = f32[4,128,128]{1,2,0:T(8,128)} async-done(((f32[4,128,128]{1,2,0:T(8,128)}), f32[4,128,128]{1,2,0:T(8,128)}) %all-reduce.9.cloned.1.call-update) | async-done | bytes 262160 | tf_op jit(solution)/shard_map/psum | solution.py:35
  814.6 1.9 fusion.6
  816.6 2.3 fusion.12
  818.9 4.4 copy.65
  823.4 143.6 %reduce-scatter.8.cloned.1.call-done = f32[4,32,128]{2,1,0:T(8,128)} async-done(((f32[256,32,128]{2,1,0:T(8,128)}), f32[4,32,128]{2,1,0:T(8,128)}) %reduce-scatter.8.cloned.1.call-update) | async-done | bytes 65552 | tf_op jit(solution)/shard_map/reduce_scatter | solution.py:21
  967.0 2.1 convolution_bitcast_fusion
  969.9 45.4 %all-reduce.11.cloned.1.call-done = f32[4,128,128]{1,2,0:T(8,128)} async-done(((f32[4,128,128]{1,2,0:T(8,128)}), f32[4,128,128]{1,2,0:T(8,128)}) %all-reduce.11.cloned.1.call-update) | async-done | bytes 262160 | tf_op jit(solution)/shard_map/psum | solution.py:35
  (82 shorter events, 26.3 us)
Async XLA Ops:
  6.5 84.4 %all-gather.10.cloned.1.call-start = ((), (), s32[]{:S(2)}) async-start(), calls=%async_computation.3 | async-start | bytes 4259840 | tf_op jit(solution)/shard_map/all_gather | solution.py:10
  8.5 117.0 %all-gather.16.cloned.1.call-start = ((), (), s32[]{:S(2)}) async-start(), calls=%async_computation.13 | async-start | bytes 1310720 | tf_op jit(solution)/shard_map/all_gather | solution.py:30
  13.2 87.2 %copy-start.5 = (f32[4,4,128,128]{3,2,1,0:T(8,128)S(1)}, f32[4,4,128,128]{3,2,1,0:T(8,128)}, u32[]{:S(2)}) copy-start(f32[4,4,128,128]{3,2,1,0:T(8,128)} %param.4) | copy-start | bytes 3145732
  91.0 6.2 copy-start.6
  97.2 29.7 %copy-start.4 = (f32[4,4,32,128]{3,2,1,0:T(8,128)S(1)}, f32[4,4,32,128]{3,2,1,0:T(8,128)}, u32[]{:S(2)}) copy-start(f32[4,4,32,128]{3,2,1,0:T(8,128)} %param.5) | copy-start | bytes 786436
  100.3 106.1 %all-gather.12.cloned.1.call-start = ((), (), s32[]{:S(2)}) async-start(), calls=%async_computation.4 | async-start | bytes 4259840 | tf_op jit(solution)/shard_map/all_gather | solution.py:10
  128.1 112.8 %all-gather.18.cloned.1.call-start = ((), (), s32[]{:S(2)}) async-start(), calls=%async_computation.14 | async-start | bytes 1310720 | tf_op jit(solution)/shard_map/all_gather | solution.py:30
  215.7 106.1 %all-gather.14.cloned.1.call-start = ((), (), s32[]{:S(2)}) async-start(), calls=%async_computation.5 | async-start | bytes 4259840 | tf_op jit(solution)/shard_map/all_gather | solution.py:10
  243.5 115.7 %all-gather.20.cloned.1.call-start = ((), (), s32[]{:S(2)}) async-start(), calls=%async_computation.15 | async-start | bytes 1310720 | tf_op jit(solution)/shard_map/all_gather | solution.py:30
  327.9 85.3 %copy-start = (f32[3,4,16,32,128]{4,3,2,1,0:T(8,128)S(1)}, f32[3,4,16,32,128]{4,3,2,1,0:T(8,128)}, u32[]{:S(2)}) copy-start(f32[3,4,16,32,128]{4,3,2,1,0:T(8,128)} %param.6) | copy-start | bytes 9437188
  334.1 79.1 %all-reduce.5.cloned.1.call-start = ((), (), s32[]{:S(2)}) async-start(), calls=%async_computation.6 | async-start | bytes 524288 | tf_op jit(solution)/shard_map/psum | solution.py:35
  365.9 199.7 %reduce-scatter.4.cloned.1.call-start = ((), (), s32[]{:S(2)}) async-start(), calls=%async_computation.7 | async-start | bytes 4259840 | tf_op jit(solution)/shard_map/reduce_scatter | solution.py:21
  421.8 143.7 %copy-start.8 = (f32[4,32,128]{2,1,0:T(8,128)S(1)}, f32[4,32,128]{2,1,0:T(8,128)}, u32[]{:S(2)}) copy-start(f32[4,32,128]{2,1,0:T(8,128)} %convolution_bitcast_fusion.7) | copy-start | bytes 196612
  421.9 192.0 %all-reduce.7.cloned.1.call-start = ((), (), s32[]{:S(2)}) async-start(), calls=%async_computation.8 | async-start | bytes 524288 | tf_op jit(solution)/shard_map/psum | solution.py:35
  567.7 198.5 %reduce-scatter.6.cloned.1.call-start = ((), (), s32[]{:S(2)}) async-start(), calls=%async_computation.9 | async-start | bytes 4259840 | tf_op jit(solution)/shard_map/reduce_scatter | solution.py:21
  622.6 143.7 %copy-start.7 = (f32[4,32,128]{2,1,0:T(8,128)S(1)}, f32[4,32,128]{2,1,0:T(8,128)}, u32[]{:S(2)}) copy-start(f32[4,32,128]{2,1,0:T(8,128)} %convolution_bitcast_fusion.8) | copy-start | bytes 196612
  622.6 192.0 %all-reduce.9.cloned.1.call-start = ((), (), s32[]{:S(2)}) async-start(), calls=%async_computation.10 | async-start | bytes 524288 | tf_op jit(solution)/shard_map/psum | solution.py:35
  768.4 198.5 %reduce-scatter.8.cloned.1.call-start = ((), (), s32[]{:S(2)}) async-start(), calls=%async_computation.11 | async-start | bytes 4259840 | tf_op jit(solution)/shard_map/reduce_scatter | solution.py:21
  823.3 143.7 %copy-start.9 = (f32[4,32,128]{2,1,0:T(8,128)S(1)}, f32[4,32,128]{2,1,0:T(8,128)}, u32[]{:S(2)}) copy-start(f32[4,32,128]{2,1,0:T(8,128)} %fusion.22) | copy-start | bytes 196612
  823.3 145.9 %copy-start.1 = (f32[4,128,128]{1,2,0:T(8,128)S(1)}, f32[4,128,128]{1,2,0:T(8,128)}, u32[]{:S(2)}) copy-start(f32[4,128,128]{1,2,0:T(8,128)} %all-reduce.5.cloned.1.call-done) | copy-start | bytes 786436
  823.3 146.1 %copy-start.2 = (f32[4,128,128]{1,2,0:T(8,128)S(1)}, f32[4,128,128]{1,2,0:T(8,128)}, u32[]{:S(2)}) copy-start(f32[4,128,128]{1,2,0:T(8,128)} %all-reduce.7.cloned.1.call-done) | copy-start | bytes 786436
  823.3 146.4 %copy-start.3 = (f32[4,128,128]{1,2,0:T(8,128)S(1)}, f32[4,128,128]{1,2,0:T(8,128)}, u32[]{:S(2)}) copy-start(f32[4,128,128]{1,2,0:T(8,128)} %all-reduce.9.cloned.1.call-done) | copy-start | bytes 786436
  823.3 192.0 %all-reduce.11.cloned.1.call-start = ((), (), s32[]{:S(2)}) async-start(), calls=%async_computation.12 | async-start | bytes 524288 | tf_op jit(solution)/shard_map/psum | solution.py:35
Sparse Core Ops, SparseCore 0:
  10.1 80.7 all-gather.9
  100.5 24.9 all-gather.15
  128.2 78.1 all-gather.11
  215.9 24.9 all-gather.17
  243.6 78.1 all-gather.13
  334.2 24.9 all-gather.19
  366.0 47.1 all-reduce.4
  422.0 143.5 reduce-scatter.3
  567.9 45.9 all-reduce.6
  622.7 143.5 reduce-scatter.5
  768.6 45.9 all-reduce.8
  823.4 143.4 reduce-scatter.7
  969.3 45.9 all-reduce.10
